TPU v7x, 32 devices: a whole 2x2x4 slice. The times are simulated.
32 devices in a mesh: tm: 16 (over z, y, x), row: 2 (over core).
Axes of the slice: x: 2, y: 2, z: 4, core: 2. Of those that a mesh axis runs over, the one named last changes fastest.
Arguments:
- initial: float32 [1024], replicated, may hold values from -6 to 6
- dynamics: float32 [1024, 1024], replicated, may hold values from -0.009765625 to 0.009765625
- obs_rows: bfloat16 [32768, 1024], P('tm', 'row'), may hold values from -0.1875 to 0.1875
- obs_values: bfloat16 [32768], P('tm'), may hold values from -6 to 6
- obs_slab: int32 [32768, 1], P('tm'), may hold values from 0 to 31; in each aligned block of 2048 rows (0 to 2047, 2048 to 4095, ...) at most 64 rows name the same one
Outputs:
- states: float32 [32, 1024], P('tm', 'row')
Inputs may be any that keep to these rules, and one draw needn't show every extreme that they name: `obs_slab`: within the rows ingested by one index of tm, no slab is named by more than 64 rows, a bound that some block reaches of them.
All inputs are finite; a program needn't handle non-finite values.
Results may differ from a plain program's by a relative error of at most 0.0003.
Values may be sent and summed in bfloat16 or wider, within the bound.
A program may use at most 128 MiB of HBM per device.

v0:
```python
import jax
import jax.numpy as jnp
from jax import lax
from jax.sharding import PartitionSpec as P

SLAB_DEV = 2
CAP = 64
sigma_gain = 0.3


def shifted(value, axis, steps):
    count = lax.axis_size(axis)
    first, last = (max(0, -steps), min(count, count - steps))
    return lax.ppermute(value, axis, [(source, source + steps) for source in range(first, last)])


def left_product(left_rows, pieces):
    new_matrix = jnp.dot(left_rows, pieces[0], precision=lax.Precision.HIGHEST)
    new_vector = jnp.dot(left_rows, pieces[1], precision=lax.Precision.HIGHEST)
    return (new_matrix, new_vector)


def body(initial, dynamics, obs_rows, obs_values, obs_slab):
    time_devs = lax.axis_size("tm")
    row_devs = lax.axis_size("row")
    state_width = dynamics.shape[1]
    local_cols = state_width // row_devs
    row_start = lax.axis_index("row") * local_cols
    time_index = lax.axis_index("tm")
    capacity = CAP
    slab_total = SLAB_DEV * time_devs
    obs_count = obs_rows.shape[0]
    target = obs_slab[:, 0]
    onehot = (target[:, None] == jnp.arange(slab_total, dtype=jnp.int32)[None, :]).astype(jnp.int32)
    rank_in = jnp.sum(onehot * (jnp.cumsum(onehot, axis=0) - 1), axis=1)
    owner_dev = target // SLAB_DEV
    within = target % SLAB_DEV
    slot_index = (within * time_devs + owner_dev) * capacity + rank_in
    slot_table = (
        jnp.full((slab_total * capacity,), obs_count, jnp.int32)
        .at[slot_index]
        .set(jnp.arange(obs_count, dtype=jnp.int32))
    )
    padded_rows = jnp.concatenate([obs_rows, jnp.zeros((1, local_cols), jnp.bfloat16)], axis=0)
    padded_values = jnp.concatenate([obs_values, jnp.zeros((1,), jnp.bfloat16)], axis=0)
    send_rows = padded_rows[slot_table].reshape(SLAB_DEV, time_devs, capacity, local_cols)
    send_values = padded_values[slot_table].reshape(SLAB_DEV, time_devs, capacity)
    recv_rows, recv_values = (
        lax.all_to_all(send_rows, "tm", split_axis=1, concat_axis=1, tiled=True),
        lax.all_to_all(send_values, "tm", split_axis=1, concat_axis=1, tiled=True),
    )
    slab_rows = recv_rows.reshape(SLAB_DEV, time_devs * capacity, local_cols)
    slab_values = recv_values.reshape(SLAB_DEV, time_devs * capacity)
    information = jnp.einsum(
        "sra,srb->sab",
        slab_rows,
        lax.all_gather(slab_rows, "row", axis=2, tiled=True),
        preferred_element_type=jnp.float32,
    )
    moment = jnp.einsum("sr,sra->sa", slab_values, slab_rows, preferred_element_type=jnp.float32)
    evolve = jnp.eye(state_width, dtype=jnp.float32) + dynamics
    evolve_rows = lax.dynamic_slice_in_dim(evolve, row_start, local_cols, 0)
    transitions = []
    offsets = []
    for slab_index in range(SLAB_DEV):
        transitions.append(
            evolve_rows
            - sigma_gain * jnp.dot(information[slab_index], evolve, precision=lax.Precision.HIGHEST)
        )
        offsets.append(sigma_gain * moment[slab_index])
    composed = transitions[0]
    composed_offset = offsets[0]
    slab_index = 1
    new_matrix, new_vector = left_product(
        transitions[slab_index],
        (
            lax.all_gather(composed, "row", axis=0, tiled=True),
            lax.all_gather(composed_offset, "row", axis=0, tiled=True),
        ),
    )
    composed = new_matrix
    composed_offset = new_vector + offsets[slab_index]
    initial_rows = lax.dynamic_slice_in_dim(initial, row_start, local_cols, 0)

    def advance(turn, state_rows):
        whole_state = lax.all_gather(state_rows, "row", axis=0, tiled=True)
        leaving = jnp.dot(composed, whole_state, precision=lax.Precision.HIGHEST) + composed_offset
        arriving = shifted(leaving, "tm", 1)
        return jnp.where(time_index == 0, initial_rows, arriving)

    entry_rows = lax.fori_loop(0, time_devs - 1, advance, initial_rows)
    states = []
    current = entry_rows
    for slab_index in range(SLAB_DEV):
        whole_state = lax.all_gather(current, "row", axis=0, tiled=True)
        current = (
            jnp.dot(transitions[slab_index], whole_state, precision=lax.Precision.HIGHEST)
            + offsets[slab_index]
        )
        states.append(current)
    return jnp.stack(states)


def solution(mesh):
    placed = (P(), P(), P("tm", "row"), P("tm"), P("tm", None))
    return jax.shard_map(
        body, mesh=mesh, in_specs=placed, out_specs=P("tm", "row"), check_vma=False
    )
```

profile of v0, /device:TPU:9, one launch (start us, length us, event | category | flops | bytes accessed | tf_op | source)
XLA Modules:
  0.0 357.0 jit_solution(5598932367776925572)
XLA Ops:
  7.3 9.1 %reduce-window.6 = s32[32,16,128]{2,1,0:T(8,128)S(1)} reduce-window(s32[32,16,128]{2,1,0:T(8,128)S(1)} %fusion.4, s32[]{:T(128)} %copy.37), window={size=1x1x128 pad=0_0x0_0x127_0}, to_apply=%region_0.0 | reduce-window | flops 8323072 | bytes 524292 | tf_op jit(solution)/shard_map/reduce-window
  17.3 8.0 %scatter_custom_fusion = s32[2048]{0:T(1024)S(1)} fusion(s32[2048]{0:T(1024)S(1)} %bitcast.110, s32[2048]{0:T(1024)S(1)} %iota.23, s32[]{:T(128)} %constant.63.clone.1), kind=kCustom, calls=%fused_computation.34 | custom fusion | bytes 8196 | tf_op jit(solution)/shard_map/scatter | solution.py:42
  27.1 9.2 %gather_fusion = bf16[2048,512]{1,0:T(8,128)(2,1)} fusion(bf16[2049,512]{1,0:T(8,128)(2,1)S(1)} %concatenate.6, s32[2048]{0:T(1024)S(1)} %fusion.5), kind=kCustom, calls=%fused_computation | custom fusion | bytes 4202496 | tf_op jit(solution)/shard_map/gather | solution.py:46
  38.2 53.8 %all_to_all.10 = bf16[2,16,64,512]{3,2,0,1:T(8,128)(2,1)S(1)} all-to-all(bf16[2,16,64,512]{3,2,0,1:T(8,128)(2,1)S(1)} %copy.17), channel_id=1, replica_groups=mesh['tm'=16,'row'=2] {'tm'}, dimensions={1} | all-to-all | bytes 4194304 | tf_op jit(solution)/shard_map/all_to_all | solution.py:49
  93.7 5.0 %convert_add_fusion = f32[1024,1024]{1,0:T(8,128)} fusion(f32[1024,1024]{1,0:T(8,128)} %param.8), kind=kLoop, calls=%fused_computation.4 | loop fusion | flops 3145728 | bytes 8388608 | tf_op jit(solution)/shard_map/add | solution.py:61
  98.6 9.4 %all-gather.9.cloned.1.call-done = bf16[2,1024,1024]{2,1,0:T(8,128)(2,1)} async-done(((bf16[2,1024,512]{2,1,0:T(8,128)(2,1)}), bf16[2,1024,1024]{2,1,0:T(8,128)(2,1)}) %all-gather.9.cloned.1.call-update) | async-done | bytes 4194320 | tf_op jit(solution)/shard_map/all_gather | solution.py:57
  108.0 4.7 %fusion.13 = f32[2,512,1024]{2,1,0:T(8,128)S(1)} fusion(bf16[2,1024,512]{2,1,0:T(8,128)(2,1)S(1)} %bitcast.86, bf16[2,1024,1024]{2,1,0:T(8,128)(2,1)} %all-gather.9.cloned.1.call-done), kind=kOutput, calls=%fused_computation.39 | convolution fusion | flops 2147483648 | bytes 10485760 | tf_op jit(solution)/shard_map/sra,srb->sab/dot_general | solution.py:54
  114.7 8.2 %multiply_subtract_fusion.1 = f32[512,1024]{1,0:T(8,128)} fusion(f32[1024,1024]{1,0:T(8,128)S(1)} %copy-done, s32[]{:T(128)S(6)} %select_n.38, f32[2,512,1024]{2,1,0:T(8,128)S(1)} %fusion.13), kind=kOutput, calls=%fused_computation.11 | convolution fusion | flops 6443499520 | bytes 10485764 | tf_op jit(solution)/shard_map/dot_general | solution.py:68
  123.6 13.1 %gather_fusion.1 = bf16[2048]{0:T(1024)(128)(2,1)S(1)} fusion(bf16[2049]{0:T(1024)(128)(2,1)S(1)} %pad_maximum_fusion, s32[2048]{0:T(1024)S(1)} %fusion.5), kind=kCustom, calls=%fused_computation.1 | custom fusion | bytes 16384 | tf_op jit(solution)/shard_map/gather | solution.py:47
  137.4 6.4 %all-to-all-start.1 = ((bf16[2,16,64]{2,0,1:T(2,128)(2,1)}), bf16[2,16,64]{2,0,1:T(2,128)(2,1)S(1)}, u32[]{:S(2)}, u32[]{:S(2)}) async-start(bf16[2,16,64]{2,0,1:T(2,128)(2,1)} %copy.20), calls=%async_computation.1 | async-start | bytes 16384 | tf_op jit(solution)/shard_map/all_to_all | solution.py:50
  143.9 5.0 %all-to-all-done.1 = bf16[2,16,64]{2,0,1:T(2,128)(2,1)S(1)} async-done(((bf16[2,16,64]{2,0,1:T(2,128)(2,1)}), bf16[2,16,64]{2,0,1:T(2,128)(2,1)S(1)}, u32[]{:S(2)}, u32[]{:S(2)}) %all-to-all-start.1) | async-done | bytes 4128 | tf_op jit(solution)/shard_map/all_to_all | solution.py:50
  149.4 3.1 all-gather
  152.5 10.1 %multiply_subtract_fusion = f32[512,1024]{1,0:T(8,128)S(1)} fusion(f32[1024,1024]{1,0:T(8,128)} %convert_add_fusion, s32[]{:T(128)S(6)} %select_n.38, f32[2,512,1024]{2,1,0:T(8,128)} %copy-done.4), kind=kOutput, calls=%fused_computation.10 | convolution fusion | flops 6443499520 | bytes 10485764 | tf_op jit(solution)/shard_map/dot_general | solution.py:68
  165.9 9.7 %fusion.14 = f32[512,1024]{1,0:T(8,128)S(1)} fusion(f32[512,1024]{1,0:T(8,128)} %copy-done.1, f32[1024,1024]{1,0:T(8,128)} %all-gather.11.cloned.1.call-done), kind=kOutput, calls=%fused_computation.40 | convolution fusion | flops 6442450944 | bytes 8388608 | tf_op jit(solution)/shard_map/dot_general | solution.py:18
  175.6 163.7 %while.12 = (s32[]{:T(128)}, f32[512]{0:T(512)S(1)}, pred[]{:T(512)}, f32[512,1024]{1,0:T(8,128)S(1)}, f32[512]{0:T(512)S(1)}, /*index=5*/f32[512]{0:T(512)S(1)}, s32[]{:T(128)}) while((s32[]{:T(128)}, f32[512]{0:T(512)S(1)}, pred[]{:T(512)}, f32[512,1024]{1,0:T(8,128)S(1)}, f32[512]{0:T(512)S(1)}, /*index=5*/f32[512]{0:T(512)S(1)}, ...), condition=%wide.region_5.6_spmd, body=%wide.region_4.5_spmd.sunk | while | flops 6292482 | bytes 2130038 | solution.py:91
  181.5 3.9 %collective-permute-done = f32[512]{0:T(512)S(1)} collective-permute-done((f32[512]{0:T(512)S(1)}, f32[512]{0:T(512)S(1)}, u32[]{:S(2)}, u32[]{:S(2)}) %collective-permute-start) | collective-permute-done | bytes 2080 | tf_op jit(solution)/shard_map/while/body/eval_jaxpr/ppermute | solution.py:14
  192.2 4.2 %collective-permute-done = f32[512]{0:T(512)S(1)} collective-permute-done((f32[512]{0:T(512)S(1)}, f32[512]{0:T(512)S(1)}, u32[]{:S(2)}, u32[]{:S(2)}) %collective-permute-start) | collective-permute-done | bytes 2080 | tf_op jit(solution)/shard_map/while/body/eval_jaxpr/ppermute | solution.py:14
  203.2 4.2 %collective-permute-done = f32[512]{0:T(512)S(1)} collective-permute-done((f32[512]{0:T(512)S(1)}, f32[512]{0:T(512)S(1)}, u32[]{:S(2)}, u32[]{:S(2)}) %collective-permute-start) | collective-permute-done | bytes 2080 | tf_op jit(solution)/shard_map/while/body/eval_jaxpr/ppermute | solution.py:14
  214.2 4.2 %collective-permute-done = f32[512]{0:T(512)S(1)} collective-permute-done((f32[512]{0:T(512)S(1)}, f32[512]{0:T(512)S(1)}, u32[]{:S(2)}, u32[]{:S(2)}) %collective-permute-start) | collective-permute-done | bytes 2080 | tf_op jit(solution)/shard_map/while/body/eval_jaxpr/ppermute | solution.py:14
  225.2 4.2 %collective-permute-done = f32[512]{0:T(512)S(1)} collective-permute-done((f32[512]{0:T(512)S(1)}, f32[512]{0:T(512)S(1)}, u32[]{:S(2)}, u32[]{:S(2)}) %collective-permute-start) | collective-permute-done | bytes 2080 | tf_op jit(solution)/shard_map/while/body/eval_jaxpr/ppermute | solution.py:14
  236.2 4.2 %collective-permute-done = f32[512]{0:T(512)S(1)} collective-permute-done((f32[512]{0:T(512)S(1)}, f32[512]{0:T(512)S(1)}, u32[]{:S(2)}, u32[]{:S(2)}) %collective-permute-start) | collective-permute-done | bytes 2080 | tf_op jit(solution)/shard_map/while/body/eval_jaxpr/ppermute | solution.py:14
  247.1 4.2 %collective-permute-done = f32[512]{0:T(512)S(1)} collective-permute-done((f32[512]{0:T(512)S(1)}, f32[512]{0:T(512)S(1)}, u32[]{:S(2)}, u32[]{:S(2)}) %collective-permute-start) | collective-permute-done | bytes 2080 | tf_op jit(solution)/shard_map/while/body/eval_jaxpr/ppermute | solution.py:14
  258.1 4.2 %collective-permute-done = f32[512]{0:T(512)S(1)} collective-permute-done((f32[512]{0:T(512)S(1)}, f32[512]{0:T(512)S(1)}, u32[]{:S(2)}, u32[]{:S(2)}) %collective-permute-start) | collective-permute-done | bytes 2080 | tf_op jit(solution)/shard_map/while/body/eval_jaxpr/ppermute | solution.py:14
  269.1 4.2 %collective-permute-done = f32[512]{0:T(512)S(1)} collective-permute-done((f32[512]{0:T(512)S(1)}, f32[512]{0:T(512)S(1)}, u32[]{:S(2)}, u32[]{:S(2)}) %collective-permute-start) | collective-permute-done | bytes 2080 | tf_op jit(solution)/shard_map/while/body/eval_jaxpr/ppermute | solution.py:14
  280.1 4.2 %collective-permute-done = f32[512]{0:T(512)S(1)} collective-permute-done((f32[512]{0:T(512)S(1)}, f32[512]{0:T(512)S(1)}, u32[]{:S(2)}, u32[]{:S(2)}) %collective-permute-start) | collective-permute-done | bytes 2080 | tf_op jit(solution)/shard_map/while/body/eval_jaxpr/ppermute | solution.py:14
  291.1 4.2 %collective-permute-done = f32[512]{0:T(512)S(1)} collective-permute-done((f32[512]{0:T(512)S(1)}, f32[512]{0:T(512)S(1)}, u32[]{:S(2)}, u32[]{:S(2)}) %collective-permute-start) | collective-permute-done | bytes 2080 | tf_op jit(solution)/shard_map/while/body/eval_jaxpr/ppermute | solution.py:14
  302.1 4.2 %collective-permute-done = f32[512]{0:T(512)S(1)} collective-permute-done((f32[512]{0:T(512)S(1)}, f32[512]{0:T(512)S(1)}, u32[]{:S(2)}, u32[]{:S(2)}) %collective-permute-start) | collective-permute-done | bytes 2080 | tf_op jit(solution)/shard_map/while/body/eval_jaxpr/ppermute | solution.py:14
  313.1 4.2 %collective-permute-done = f32[512]{0:T(512)S(1)} collective-permute-done((f32[512]{0:T(512)S(1)}, f32[512]{0:T(512)S(1)}, u32[]{:S(2)}, u32[]{:S(2)}) %collective-permute-start) | collective-permute-done | bytes 2080 | tf_op jit(solution)/shard_map/while/body/eval_jaxpr/ppermute | solution.py:14
  324.0 4.2 %collective-permute-done = f32[512]{0:T(512)S(1)} collective-permute-done((f32[512]{0:T(512)S(1)}, f32[512]{0:T(512)S(1)}, u32[]{:S(2)}, u32[]{:S(2)}) %collective-permute-start) | collective-permute-done | bytes 2080 | tf_op jit(solution)/shard_map/while/body/eval_jaxpr/ppermute | solution.py:14
  335.0 4.2 %collective-permute-done = f32[512]{0:T(512)S(1)} collective-permute-done((f32[512]{0:T(512)S(1)}, f32[512]{0:T(512)S(1)}, u32[]{:S(2)}, u32[]{:S(2)}) %collective-permute-start) | collective-permute-done | bytes 2080 | tf_op jit(solution)/shard_map/while/body/eval_jaxpr/ppermute | solution.py:14
  339.2 3.1 all-gather.2
  342.3 3.4 fusion.16
  (125 shorter events, 119.1 us)
Async XLA Ops:
  6.5 10.6 %copy-start.5 = (s32[2048,1]{0,1:T(1,128)S(1)}, s32[2048,1]{0,1:T(1,128)}, u32[]{:S(2)}) copy-start(s32[2048,1]{0,1:T(1,128)} %param.11) | copy-start | bytes 24580
  6.5 101.5 %all-gather.9.cloned.1.call-start = ((), (), s32[]{:S(2)}) async-start(), calls=%async_computation.2 | async-start | bytes 6291456 | tf_op jit(solution)/shard_map/all_gather | solution.py:57
  93.6 72.3 %all-gather.11.cloned.1.call-start = ((), (), s32[]{:S(2)}) async-start(), calls=%async_computation.3 | async-start | bytes 6291456 | tf_op jit(solution)/shard_map/all_gather | solution.py:77
  93.7 14.4 %copy-start.3 = (bf16[2,16,64,512]{3,2,1,0:T(8,128)(2,1)S(1)}, bf16[2,16,64,512]{3,2,1,0:T(8,128)(2,1)}, u32[]{:S(2)}) copy-start(bf16[2,16,64,512]{3,2,1,0:T(8,128)(2,1)} %copy.18) | copy-start | bytes 6291460
  108.0 6.7 %copy-start = (f32[1024,1024]{1,0:T(8,128)S(1)}, f32[1024,1024]{1,0:T(8,128)}, u32[]{:S(2)}) copy-start(f32[1024,1024]{1,0:T(8,128)} %convert_add_fusion) | copy-start | bytes 12582916
  112.7 2.0 copy-start.4
  123.0 0.7 copy-start.6
  123.6 20.2 %copy-start.7 = (f32[1024]{0:T(1024)S(1)}, f32[1024]{0:T(1024)}, u32[]{:S(2)}) copy-start(f32[1024]{0:T(1024)} %param.7) | copy-start | bytes 12292
  137.4 11.5 %all-to-all-start.1 = ((bf16[2,16,64]{2,0,1:T(2,128)(2,1)}), bf16[2,16,64]{2,0,1:T(2,128)(2,1)S(1)}, u32[]{:S(2)}, u32[]{:S(2)}) async-start(bf16[2,16,64]{2,0,1:T(2,128)(2,1)} %copy.20), calls=%async_computation.1 | async-start | bytes 16384 | tf_op jit(solution)/shard_map/all_to_all | solution.py:50
  162.7 1.3 copy-start.1
  179.3 6.1 %collective-permute-start = (f32[512]{0:T(512)S(1)}, f32[512]{0:T(512)S(1)}, u32[]{:S(2)}, u32[]{:S(2)}) collective-permute-start(f32[512]{0:T(512)S(1)} %add.85), channel_id=1, source_target_pairs={{0,2},{2,4},{4,6},{6,8},{8,10},{10,12},{12,14},{14,16},{16,18},{18... | collective-permute-start | bytes 6152 | tf_op jit(solution)/shard_map/while/body/eval_jaxpr/ppermute | solution.py:14
  190.3 6.1 %collective-permute-start = (f32[512]{0:T(512)S(1)}, f32[512]{0:T(512)S(1)}, u32[]{:S(2)}, u32[]{:S(2)}) collective-permute-start(f32[512]{0:T(512)S(1)} %add.85), channel_id=1, source_target_pairs={{0,2},{2,4},{4,6},{6,8},{8,10},{10,12},{12,14},{14,16},{16,18},{18... | collective-permute-start | bytes 6152 | tf_op jit(solution)/shard_map/while/body/eval_jaxpr/ppermute | solution.py:14
  201.3 6.1 %collective-permute-start = (f32[512]{0:T(512)S(1)}, f32[512]{0:T(512)S(1)}, u32[]{:S(2)}, u32[]{:S(2)}) collective-permute-start(f32[512]{0:T(512)S(1)} %add.85), channel_id=1, source_target_pairs={{0,2},{2,4},{4,6},{6,8},{8,10},{10,12},{12,14},{14,16},{16,18},{18... | collective-permute-start | bytes 6152 | tf_op jit(solution)/shard_map/while/body/eval_jaxpr/ppermute | solution.py:14
  212.2 6.1 %collective-permute-start = (f32[512]{0:T(512)S(1)}, f32[512]{0:T(512)S(1)}, u32[]{:S(2)}, u32[]{:S(2)}) collective-permute-start(f32[512]{0:T(512)S(1)} %add.85), channel_id=1, source_target_pairs={{0,2},{2,4},{4,6},{6,8},{8,10},{10,12},{12,14},{14,16},{16,18},{18... | collective-permute-start | bytes 6152 | tf_op jit(solution)/shard_map/while/body/eval_jaxpr/ppermute | solution.py:14
  223.2 6.1 %collective-permute-start = (f32[512]{0:T(512)S(1)}, f32[512]{0:T(512)S(1)}, u32[]{:S(2)}, u32[]{:S(2)}) collective-permute-start(f32[512]{0:T(512)S(1)} %add.85), channel_id=1, source_target_pairs={{0,2},{2,4},{4,6},{6,8},{8,10},{10,12},{12,14},{14,16},{16,18},{18... | collective-permute-start | bytes 6152 | tf_op jit(solution)/shard_map/while/body/eval_jaxpr/ppermute | solution.py:14
  234.2 6.1 %collective-permute-start = (f32[512]{0:T(512)S(1)}, f32[512]{0:T(512)S(1)}, u32[]{:S(2)}, u32[]{:S(2)}) collective-permute-start(f32[512]{0:T(512)S(1)} %add.85), channel_id=1, source_target_pairs={{0,2},{2,4},{4,6},{6,8},{8,10},{10,12},{12,14},{14,16},{16,18},{18... | collective-permute-start | bytes 6152 | tf_op jit(solution)/shard_map/while/body/eval_jaxpr/ppermute | solution.py:14
  245.2 6.1 %collective-permute-start = (f32[512]{0:T(512)S(1)}, f32[512]{0:T(512)S(1)}, u32[]{:S(2)}, u32[]{:S(2)}) collective-permute-start(f32[512]{0:T(512)S(1)} %add.85), channel_id=1, source_target_pairs={{0,2},{2,4},{4,6},{6,8},{8,10},{10,12},{12,14},{14,16},{16,18},{18... | collective-permute-start | bytes 6152 | tf_op jit(solution)/shard_map/while/body/eval_jaxpr/ppermute | solution.py:14
  256.2 6.1 %collective-permute-start = (f32[512]{0:T(512)S(1)}, f32[512]{0:T(512)S(1)}, u32[]{:S(2)}, u32[]{:S(2)}) collective-permute-start(f32[512]{0:T(512)S(1)} %add.85), channel_id=1, source_target_pairs={{0,2},{2,4},{4,6},{6,8},{8,10},{10,12},{12,14},{14,16},{16,18},{18... | collective-permute-start | bytes 6152 | tf_op jit(solution)/shard_map/while/body/eval_jaxpr/ppermute | solution.py:14
  267.2 6.1 %collective-permute-start = (f32[512]{0:T(512)S(1)}, f32[512]{0:T(512)S(1)}, u32[]{:S(2)}, u32[]{:S(2)}) collective-permute-start(f32[512]{0:T(512)S(1)} %add.85), channel_id=1, source_target_pairs={{0,2},{2,4},{4,6},{6,8},{8,10},{10,12},{12,14},{14,16},{16,18},{18... | collective-permute-start | bytes 6152 | tf_op jit(solution)/shard_map/while/body/eval_jaxpr/ppermute | solution.py:14
  278.2 6.1 %collective-permute-start = (f32[512]{0:T(512)S(1)}, f32[512]{0:T(512)S(1)}, u32[]{:S(2)}, u32[]{:S(2)}) collective-permute-start(f32[512]{0:T(512)S(1)} %add.85), channel_id=1, source_target_pairs={{0,2},{2,4},{4,6},{6,8},{8,10},{10,12},{12,14},{14,16},{16,18},{18... | collective-permute-start | bytes 6152 | tf_op jit(solution)/shard_map/while/body/eval_jaxpr/ppermute | solution.py:14
  289.1 6.1 %collective-permute-start = (f32[512]{0:T(512)S(1)}, f32[512]{0:T(512)S(1)}, u32[]{:S(2)}, u32[]{:S(2)}) collective-permute-start(f32[512]{0:T(512)S(1)} %add.85), channel_id=1, source_target_pairs={{0,2},{2,4},{4,6},{6,8},{8,10},{10,12},{12,14},{14,16},{16,18},{18... | collective-permute-start | bytes 6152 | tf_op jit(solution)/shard_map/while/body/eval_jaxpr/ppermute | solution.py:14
  300.1 6.1 %collective-permute-start = (f32[512]{0:T(512)S(1)}, f32[512]{0:T(512)S(1)}, u32[]{:S(2)}, u32[]{:S(2)}) collective-permute-start(f32[512]{0:T(512)S(1)} %add.85), channel_id=1, source_target_pairs={{0,2},{2,4},{4,6},{6,8},{8,10},{10,12},{12,14},{14,16},{16,18},{18... | collective-permute-start | bytes 6152 | tf_op jit(solution)/shard_map/while/body/eval_jaxpr/ppermute | solution.py:14
  311.1 6.1 %collective-permute-start = (f32[512]{0:T(512)S(1)}, f32[512]{0:T(512)S(1)}, u32[]{:S(2)}, u32[]{:S(2)}) collective-permute-start(f32[512]{0:T(512)S(1)} %add.85), channel_id=1, source_target_pairs={{0,2},{2,4},{4,6},{6,8},{8,10},{10,12},{12,14},{14,16},{16,18},{18... | collective-permute-start | bytes 6152 | tf_op jit(solution)/shard_map/while/body/eval_jaxpr/ppermute | solution.py:14
  322.1 6.1 %collective-permute-start = (f32[512]{0:T(512)S(1)}, f32[512]{0:T(512)S(1)}, u32[]{:S(2)}, u32[]{:S(2)}) collective-permute-start(f32[512]{0:T(512)S(1)} %add.85), channel_id=1, source_target_pairs={{0,2},{2,4},{4,6},{6,8},{8,10},{10,12},{12,14},{14,16},{16,18},{18... | collective-permute-start | bytes 6152 | tf_op jit(solution)/shard_map/while/body/eval_jaxpr/ppermute | solution.py:14
  333.1 6.1 %collective-permute-start = (f32[512]{0:T(512)S(1)}, f32[512]{0:T(512)S(1)}, u32[]{:S(2)}, u32[]{:S(2)}) collective-permute-start(f32[512]{0:T(512)S(1)} %add.85), channel_id=1, source_target_pairs={{0,2},{2,4},{4,6},{6,8},{8,10},{10,12},{12,14},{14,16},{16,18},{18... | collective-permute-start | bytes 6152 | tf_op jit(solution)/shard_map/while/body/eval_jaxpr/ppermute | solution.py:14
  339.2 8.4 %copy-start.2 = (f32[512,1024]{1,0:T(8,128)S(1)}, f32[512,1024]{1,0:T(8,128)}, u32[]{:S(2)}) copy-start(f32[512,1024]{1,0:T(8,128)} %copy-done.1) | copy-start | bytes 6291460
Sparse Core Ops, SparseCore 0:
  93.7 14.2 all-gather.8
  123.1 14.8 all-gather.10
where the time goes:
time: 358 us; the launch traced here: 357 us
  blocking collectives  105 us (29%)
  waiting for transfers between devices  77.1 us (22%)
  matrix products  68.2 us (19%)
  local copies, waits for them, and re-layouts  40.7 us (11%)
  starting transfers between devices  35.6 us (10%)
  other arithmetic  16.2 us (5%)
  between operations  13.6 us (4%)
    ppermute x15, waiting for transfers between devices, shifted(): lax.ppermute(value, axis, [(source, source + steps) for source in range(f...  62.7 us
    all_to_all x1, blocking collectives, body(): lax.all_to_all(send_rows, 'tm', split_axis=1, concat_axis=1, tiled=True)  53.8 us
    all_gather x15, blocking collectives, advance(): whole_state = lax.all_gather(state_rows, 'row', axis=0, tiled=True)  43.5 us
    ppermute x15, starting transfers between devices, shifted(): lax.ppermute(value, axis, [(source, source + steps) for source in range(f...  29.1 us
    dot_general x15, matrix products, advance(): jnp.dot(composed, whole_state, precision=lax.Precision.HIGHEST)  28 us
    dot_general x2, matrix products, body(): jnp.dot(information[slab_index], evolve, precision=lax.Precision.HIGHEST)  18.4 us
    gather x1, local copies, waits for them, and re-layouts, body(): padded_values[slot_table].reshape(SLAB_DEV, time_devs, capacity)  13.1 us
    dot_general x1, matrix products, left_product(): new_matrix = jnp.dot(left_rows, pieces[0], precision=lax.Precision.HIGHEST)  9.65 us
  transfers between devices with their start and end apart: 18, of which 17 were waited for; matrix products, arithmetic and copies ran while one was open for 9% of the time, Pallas kernels for 0%

commit v1 on v0

--- a/solution.py
+++ b/solution.py
@@ -83,7 +83,9 @@
     initial_rows = lax.dynamic_slice_in_dim(initial, row_start, local_cols, 0)
 
     def advance(turn, state_rows):
-        whole_state = lax.all_gather(state_rows, "row", axis=0, tiled=True)
+        whole_state = jnp.concatenate(
+            lax.all_to_all(jnp.stack([state_rows] * lax.axis_size("row")), "row", 0, 0), axis=0
+        )
         leaving = jnp.dot(composed, whole_state, precision=lax.Precision.HIGHEST) + composed_offset
         arriving = shifted(leaving, "tm", 1)
         return jnp.where(time_index == 0, initial_rows, arriving)

time: 358 us -> 386 us (1.078)
  blocking collectives: 105 us -> 134 us
    all_to_all x0 -> x15, blocking collectives: none -> 71.6 us  [advance(): lax.all_to_all(jnp.stack([state_rows] * lax.axis_size('row')), 'row', 0, 0)]
    all_gather x15 -> x0, blocking collectives: 43.5 us -> none  [advance(): whole_state = lax.all_gather(state_rows, 'row', axis=0, tiled=True)]
    another operation x2 -> x17, other arithmetic: 9.27 us -> 9.44 us
  transfers between devices with their start and end apart: 18 -> 18, of which waited for: 17 -> 17; matrix products, arithmetic and copies ran while one was open for 9% -> 8% of each run, Pallas kernels for 0% -> 0%
where the time goes in v1:
time: 386 us; the launch traced here: 385 us
  blocking collectives  134 us (35%)
  waiting for transfers between devices  77.1 us (20%)
  matrix products  67.5 us (17%)
  local copies, waits for them, and re-layouts  40.8 us (11%)
  starting transfers between devices  35.6 us (9%)
  other arithmetic  16.3 us (4%)
  between operations  13.6 us (4%)
    all_to_all x15, blocking collectives, advance(): lax.all_to_all(jnp.stack([state_rows] * lax.axis_size('row')), 'row', 0, 0)  71.6 us
    ppermute x15, waiting for transfers between devices, shifted(): lax.ppermute(value, axis, [(source, source + steps) for source in range(f...  62.7 us
    all_to_all x1, blocking collectives, body(): lax.all_to_all(send_rows, 'tm', split_axis=1, concat_axis=1, tiled=True)  53.8 us
    ppermute x15, starting transfers between devices, shifted(): lax.ppermute(value, axis, [(source, source + steps) for source in range(f...  29.1 us
    dot_general x15, matrix products, advance(): jnp.dot(composed, whole_state, precision=lax.Precision.HIGHEST)  27.2 us
    dot_general x2, matrix products, body(): jnp.dot(information[slab_index], evolve, precision=lax.Precision.HIGHEST)  18.4 us
    gather x1, local copies, waits for them, and re-layouts, body(): padded_values[slot_table].reshape(SLAB_DEV, time_devs, capacity)  13.1 us
    dot_general x1, matrix products, left_product(): new_matrix = jnp.dot(left_rows, pieces[0], precision=lax.Precision.HIGHEST)  9.65 us
  transfers between devices with their start and end apart: 18, of which 17 were waited for; matrix products, arithmetic and copies ran while one was open for 8% of the time, Pallas kernels for 0%

profile of v1, /device:TPU:9, one launch (start us, length us, event | category | flops | bytes accessed | tf_op | source)
XLA Modules:
  0.0 384.6 jit_solution(9978014133052833046)
XLA Ops:
  7.3 9.1 %reduce-window.6 = s32[32,16,128]{2,1,0:T(8,128)S(1)} reduce-window(s32[32,16,128]{2,1,0:T(8,128)S(1)} %fusion.4, s32[]{:T(128)} %copy.37), window={size=1x1x128 pad=0_0x0_0x127_0}, to_apply=%region_0.0 | reduce-window | flops 8323072 | bytes 524292 | tf_op jit(solution)/shard_map/reduce-window
  17.3 8.0 %scatter_custom_fusion = s32[2048]{0:T(1024)S(1)} fusion(s32[2048]{0:T(1024)S(1)} %bitcast.110, s32[2048]{0:T(1024)S(1)} %iota.23, s32[]{:T(128)} %constant.63.clone.1), kind=kCustom, calls=%fused_computation.35 | custom fusion | bytes 8196 | tf_op jit(solution)/shard_map/scatter | solution.py:42
  27.1 9.2 %gather_fusion = bf16[2048,512]{1,0:T(8,128)(2,1)} fusion(bf16[2049,512]{1,0:T(8,128)(2,1)S(1)} %concatenate.6, s32[2048]{0:T(1024)S(1)} %fusion.5), kind=kCustom, calls=%fused_computation | custom fusion | bytes 4202496 | tf_op jit(solution)/shard_map/gather | solution.py:46
  38.2 53.8 %all_to_all.23 = bf16[2,16,64,512]{3,2,0,1:T(8,128)(2,1)S(1)} all-to-all(bf16[2,16,64,512]{3,2,0,1:T(8,128)(2,1)S(1)} %copy.17), channel_id=1, replica_groups=mesh['tm'=16,'row'=2] {'tm'}, dimensions={1} | all-to-all | bytes 4194304 | tf_op jit(solution)/shard_map/all_to_all | solution.py:49
  93.7 5.0 %convert_add_fusion = f32[1024,1024]{1,0:T(8,128)} fusion(f32[1024,1024]{1,0:T(8,128)} %param.8), kind=kLoop, calls=%fused_computation.5 | loop fusion | flops 3145728 | bytes 8388608 | tf_op jit(solution)/shard_map/add | solution.py:61
  98.6 9.4 %all-gather.6.cloned.1.call-done = bf16[2,1024,1024]{2,1,0:T(8,128)(2,1)} async-done(((bf16[2,1024,512]{2,1,0:T(8,128)(2,1)}), bf16[2,1024,1024]{2,1,0:T(8,128)(2,1)}) %all-gather.6.cloned.1.call-update) | async-done | bytes 4194320 | tf_op jit(solution)/shard_map/all_gather | solution.py:57
  108.0 4.7 %fusion.13 = f32[2,512,1024]{2,1,0:T(8,128)S(1)} fusion(bf16[2,1024,512]{2,1,0:T(8,128)(2,1)S(1)} %bitcast.86, bf16[2,1024,1024]{2,1,0:T(8,128)(2,1)} %all-gather.6.cloned.1.call-done), kind=kOutput, calls=%fused_computation.40 | convolution fusion | flops 2147483648 | bytes 10485760 | tf_op jit(solution)/shard_map/sra,srb->sab/dot_general | solution.py:54
  114.7 8.2 %multiply_subtract_fusion.1 = f32[512,1024]{1,0:T(8,128)} fusion(f32[1024,1024]{1,0:T(8,128)S(1)} %copy-done, s32[]{:T(128)S(6)} %select_n.38, f32[2,512,1024]{2,1,0:T(8,128)S(1)} %fusion.13), kind=kOutput, calls=%fused_computation.12 | convolution fusion | flops 6443499520 | bytes 10485764 | tf_op jit(solution)/shard_map/dot_general | solution.py:68
  123.6 13.1 %gather_fusion.1 = bf16[2048]{0:T(1024)(128)(2,1)S(1)} fusion(bf16[2049]{0:T(1024)(128)(2,1)S(1)} %pad_maximum_fusion.1, s32[2048]{0:T(1024)S(1)} %fusion.5), kind=kCustom, calls=%fused_computation.1 | custom fusion | bytes 16384 | tf_op jit(solution)/shard_map/gather | solution.py:47
  137.4 6.4 %all-to-all-start.2 = ((bf16[2,16,64]{2,0,1:T(2,128)(2,1)}), bf16[2,16,64]{2,0,1:T(2,128)(2,1)S(1)}, u32[]{:S(2)}, u32[]{:S(2)}) async-start(bf16[2,16,64]{2,0,1:T(2,128)(2,1)} %copy.20), calls=%async_computation.2 | async-start | bytes 16384 | tf_op jit(solution)/shard_map/all_to_all | solution.py:50
  143.9 5.0 %all-to-all-done.2 = bf16[2,16,64]{2,0,1:T(2,128)(2,1)S(1)} async-done(((bf16[2,16,64]{2,0,1:T(2,128)(2,1)}), bf16[2,16,64]{2,0,1:T(2,128)(2,1)S(1)}, u32[]{:S(2)}, u32[]{:S(2)}) %all-to-all-start.2) | async-done | bytes 4128 | tf_op jit(solution)/shard_map/all_to_all | solution.py:50
  152.5 10.1 %multiply_subtract_fusion = f32[512,1024]{1,0:T(8,128)S(1)} fusion(f32[1024,1024]{1,0:T(8,128)} %convert_add_fusion, s32[]{:T(128)S(6)} %select_n.38, f32[2,512,1024]{2,1,0:T(8,128)} %copy-done.4), kind=kOutput, calls=%fused_computation.11 | convolution fusion | flops 6443499520 | bytes 10485764 | tf_op jit(solution)/shard_map/dot_general | solution.py:68
  165.9 9.7 %fusion.14 = f32[512,1024]{1,0:T(8,128)S(1)} fusion(f32[512,1024]{1,0:T(8,128)} %copy-done.1, f32[1024,1024]{1,0:T(8,128)} %all-gather.8.cloned.1.call-done), kind=kOutput, calls=%fused_computation.41 | convolution fusion | flops 6442450944 | bytes 8388608 | tf_op jit(solution)/shard_map/dot_general | solution.py:18
  175.6 191.3 %while.12 = (s32[]{:T(128)}, f32[512]{0:T(512)S(1)}, pred[]{:T(512)}, f32[512,1024]{1,0:T(8,128)S(1)}, f32[512]{0:T(512)S(1)}, /*index=5*/f32[512]{0:T(512)S(1)}, s32[]{:T(128)}) while((s32[]{:T(128)}, f32[512]{0:T(512)S(1)}, pred[]{:T(512)}, f32[512,1024]{1,0:T(8,128)S(1)}, f32[512]{0:T(512)S(1)}, /*index=5*/f32[512]{0:T(512)S(1)}, ...), condition=%wide.region_5.6_spmd, body=%wide.region_4.5_spmd.sunk | while | flops 6293506 | bytes 2146422 | solution.py:93
  187.3 4.8 %all_to_all.24 = f32[2,1,512]{2,1,0:T(1,128)S(1)} all-to-all(f32[2,1,512]{2,1,0:T(1,128)S(1)} %all_to_all.18), channel_id=1, replica_groups=mesh['tm'=16,'row'=2] {'row'}, dimensions={0} | all-to-all | bytes 8192 | tf_op jit(solution)/shard_map/while/body/eval_jaxpr/all_to_all | solution.py:87
  195.9 4.2 %collective-permute-done = f32[512]{0:T(512)S(1)} collective-permute-done((f32[512]{0:T(512)S(1)}, f32[512]{0:T(512)S(1)}, u32[]{:S(2)}, u32[]{:S(2)}) %collective-permute-start) | collective-permute-done | bytes 2080 | tf_op jit(solution)/shard_map/while/body/eval_jaxpr/ppermute | solution.py:14
  200.1 4.8 %all_to_all.24 = f32[2,1,512]{2,1,0:T(1,128)S(1)} all-to-all(f32[2,1,512]{2,1,0:T(1,128)S(1)} %all_to_all.18), channel_id=1, replica_groups=mesh['tm'=16,'row'=2] {'row'}, dimensions={0} | all-to-all | bytes 8192 | tf_op jit(solution)/shard_map/while/body/eval_jaxpr/all_to_all | solution.py:87
  208.7 4.2 %collective-permute-done = f32[512]{0:T(512)S(1)} collective-permute-done((f32[512]{0:T(512)S(1)}, f32[512]{0:T(512)S(1)}, u32[]{:S(2)}, u32[]{:S(2)}) %collective-permute-start) | collective-permute-done | bytes 2080 | tf_op jit(solution)/shard_map/while/body/eval_jaxpr/ppermute | solution.py:14
  212.9 4.8 %all_to_all.24 = f32[2,1,512]{2,1,0:T(1,128)S(1)} all-to-all(f32[2,1,512]{2,1,0:T(1,128)S(1)} %all_to_all.18), channel_id=1, replica_groups=mesh['tm'=16,'row'=2] {'row'}, dimensions={0} | all-to-all | bytes 8192 | tf_op jit(solution)/shard_map/while/body/eval_jaxpr/all_to_all | solution.py:87
  221.5 4.2 %collective-permute-done = f32[512]{0:T(512)S(1)} collective-permute-done((f32[512]{0:T(512)S(1)}, f32[512]{0:T(512)S(1)}, u32[]{:S(2)}, u32[]{:S(2)}) %collective-permute-start) | collective-permute-done | bytes 2080 | tf_op jit(solution)/shard_map/while/body/eval_jaxpr/ppermute | solution.py:14
  225.8 4.8 %all_to_all.24 = f32[2,1,512]{2,1,0:T(1,128)S(1)} all-to-all(f32[2,1,512]{2,1,0:T(1,128)S(1)} %all_to_all.18), channel_id=1, replica_groups=mesh['tm'=16,'row'=2] {'row'}, dimensions={0} | all-to-all | bytes 8192 | tf_op jit(solution)/shard_map/while/body/eval_jaxpr/all_to_all | solution.py:87
  234.4 4.2 %collective-permute-done = f32[512]{0:T(512)S(1)} collective-permute-done((f32[512]{0:T(512)S(1)}, f32[512]{0:T(512)S(1)}, u32[]{:S(2)}, u32[]{:S(2)}) %collective-permute-start) | collective-permute-done | bytes 2080 | tf_op jit(solution)/shard_map/while/body/eval_jaxpr/ppermute | solution.py:14
  238.6 4.8 %all_to_all.24 = f32[2,1,512]{2,1,0:T(1,128)S(1)} all-to-all(f32[2,1,512]{2,1,0:T(1,128)S(1)} %all_to_all.18), channel_id=1, replica_groups=mesh['tm'=16,'row'=2] {'row'}, dimensions={0} | all-to-all | bytes 8192 | tf_op jit(solution)/shard_map/while/body/eval_jaxpr/all_to_all | solution.py:87
  251.4 4.8 %all_to_all.24 = f32[2,1,512]{2,1,0:T(1,128)S(1)} all-to-all(f32[2,1,512]{2,1,0:T(1,128)S(1)} %all_to_all.18), channel_id=1, replica_groups=mesh['tm'=16,'row'=2] {'row'}, dimensions={0} | all-to-all | bytes 8192 | tf_op jit(solution)/shard_map/while/body/eval_jaxpr/all_to_all | solution.py:87
  264.3 4.8 %all_to_all.24 = f32[2,1,512]{2,1,0:T(1,128)S(1)} all-to-all(f32[2,1,512]{2,1,0:T(1,128)S(1)} %all_to_all.18), channel_id=1, replica_groups=mesh['tm'=16,'row'=2] {'row'}, dimensions={0} | all-to-all | bytes 8192 | tf_op jit(solution)/shard_map/while/body/eval_jaxpr/all_to_all | solution.py:87
  277.1 4.8 %all_to_all.24 = f32[2,1,512]{2,1,0:T(1,128)S(1)} all-to-all(f32[2,1,512]{2,1,0:T(1,128)S(1)} %all_to_all.18), channel_id=1, replica_groups=mesh['tm'=16,'row'=2] {'row'}, dimensions={0} | all-to-all | bytes 8192 | tf_op jit(solution)/shard_map/while/body/eval_jaxpr/all_to_all | solution.py:87
  289.9 4.8 %all_to_all.24 = f32[2,1,512]{2,1,0:T(1,128)S(1)} all-to-all(f32[2,1,512]{2,1,0:T(1,128)S(1)} %all_to_all.18), channel_id=1, replica_groups=mesh['tm'=16,'row'=2] {'row'}, dimensions={0} | all-to-all | bytes 8192 | tf_op jit(solution)/shard_map/while/body/eval_jaxpr/all_to_all | solution.py:87
  302.8 4.8 %all_to_all.24 = f32[2,1,512]{2,1,0:T(1,128)S(1)} all-to-all(f32[2,1,512]{2,1,0:T(1,128)S(1)} %all_to_all.18), channel_id=1, replica_groups=mesh['tm'=16,'row'=2] {'row'}, dimensions={0} | all-to-all | bytes 8192 | tf_op jit(solution)/shard_map/while/body/eval_jaxpr/all_to_all | solution.py:87
  315.6 4.8 %all_to_all.24 = f32[2,1,512]{2,1,0:T(1,128)S(1)} all-to-all(f32[2,1,512]{2,1,0:T(1,128)S(1)} %all_to_all.18), channel_id=1, replica_groups=mesh['tm'=16,'row'=2] {'row'}, dimensions={0} | all-to-all | bytes 8192 | tf_op jit(solution)/shard_map/while/body/eval_jaxpr/all_to_all | solution.py:87
  328.4 4.8 %all_to_all.24 = f32[2,1,512]{2,1,0:T(1,128)S(1)} all-to-all(f32[2,1,512]{2,1,0:T(1,128)S(1)} %all_to_all.18), channel_id=1, replica_groups=mesh['tm'=16,'row'=2] {'row'}, dimensions={0} | all-to-all | bytes 8192 | tf_op jit(solution)/shard_map/while/body/eval_jaxpr/all_to_all | solution.py:87
  341.2 4.8 %all_to_all.24 = f32[2,1,512]{2,1,0:T(1,128)S(1)} all-to-all(f32[2,1,512]{2,1,0:T(1,128)S(1)} %all_to_all.18), channel_id=1, replica_groups=mesh['tm'=16,'row'=2] {'row'}, dimensions={0} | all-to-all | bytes 8192 | tf_op jit(solution)/shard_map/while/body/eval_jaxpr/all_to_all | solution.py:87
  354.1 4.8 %all_to_all.24 = f32[2,1,512]{2,1,0:T(1,128)S(1)} all-to-all(f32[2,1,512]{2,1,0:T(1,128)S(1)} %all_to_all.18), channel_id=1, replica_groups=mesh['tm'=16,'row'=2] {'row'}, dimensions={0} | all-to-all | bytes 8192 | tf_op jit(solution)/shard_map/while/body/eval_jaxpr/all_to_all | solution.py:87
  (155 shorter events, 134.4 us)
Async XLA Ops:
  6.5 10.6 %copy-start.5 = (s32[2048,1]{0,1:T(1,128)S(1)}, s32[2048,1]{0,1:T(1,128)}, u32[]{:S(2)}) copy-start(s32[2048,1]{0,1:T(1,128)} %param.11) | copy-start | bytes 24580
  6.5 101.5 %all-gather.6.cloned.1.call-start = ((), (), s32[]{:S(2)}) async-start(), calls=%async_computation.3 | async-start | bytes 6291456 | tf_op jit(solution)/shard_map/all_gather | solution.py:57
  93.6 72.3 %all-gather.8.cloned.1.call-start = ((), (), s32[]{:S(2)}) async-start(), calls=%async_computation.4 | async-start | bytes 6291456 | tf_op jit(solution)/shard_map/all_gather | solution.py:77
  93.7 14.4 %copy-start.3 = (bf16[2,16,64,512]{3,2,1,0:T(8,128)(2,1)S(1)}, bf16[2,16,64,512]{3,2,1,0:T(8,128)(2,1)}, u32[]{:S(2)}) copy-start(bf16[2,16,64,512]{3,2,1,0:T(8,128)(2,1)} %copy.18) | copy-start | bytes 6291460
  108.0 6.7 %copy-start = (f32[1024,1024]{1,0:T(8,128)S(1)}, f32[1024,1024]{1,0:T(8,128)}, u32[]{:S(2)}) copy-start(f32[1024,1024]{1,0:T(8,128)} %convert_add_fusion) | copy-start | bytes 12582916
  112.7 2.0 copy-start.4
  123.0 0.7 copy-start.6
  123.6 20.2 %copy-start.7 = (f32[1024]{0:T(1024)S(1)}, f32[1024]{0:T(1024)}, u32[]{:S(2)}) copy-start(f32[1024]{0:T(1024)} %param.7) | copy-start | bytes 12292
  137.4 11.5 %all-to-all-start.2 = ((bf16[2,16,64]{2,0,1:T(2,128)(2,1)}), bf16[2,16,64]{2,0,1:T(2,128)(2,1)S(1)}, u32[]{:S(2)}, u32[]{:S(2)}) async-start(bf16[2,16,64]{2,0,1:T(2,128)(2,1)} %copy.20), calls=%async_computation.2 | async-start | bytes 16384 | tf_op jit(solution)/shard_map/all_to_all | solution.py:50
  162.7 1.3 copy-start.1
  181.1 6.1 %collective-permute-start = (f32[512]{0:T(512)S(1)}, f32[512]{0:T(512)S(1)}, u32[]{:S(2)}, u32[]{:S(2)}) collective-permute-start(f32[512]{0:T(512)S(1)} %add.85), channel_id=1, source_target_pairs={{0,2},{2,4},{4,6},{6,8},{8,10},{10,12},{12,14},{14,16},{16,18},{18... | collective-permute-start | bytes 6152 | tf_op jit(solution)/shard_map/while/body/eval_jaxpr/ppermute | solution.py:14
  194.0 6.1 %collective-permute-start = (f32[512]{0:T(512)S(1)}, f32[512]{0:T(512)S(1)}, u32[]{:S(2)}, u32[]{:S(2)}) collective-permute-start(f32[512]{0:T(512)S(1)} %add.85), channel_id=1, source_target_pairs={{0,2},{2,4},{4,6},{6,8},{8,10},{10,12},{12,14},{14,16},{16,18},{18... | collective-permute-start | bytes 6152 | tf_op jit(solution)/shard_map/while/body/eval_jaxpr/ppermute | solution.py:14
  206.8 6.1 %collective-permute-start = (f32[512]{0:T(512)S(1)}, f32[512]{0:T(512)S(1)}, u32[]{:S(2)}, u32[]{:S(2)}) collective-permute-start(f32[512]{0:T(512)S(1)} %add.85), channel_id=1, source_target_pairs={{0,2},{2,4},{4,6},{6,8},{8,10},{10,12},{12,14},{14,16},{16,18},{18... | collective-permute-start | bytes 6152 | tf_op jit(solution)/shard_map/while/body/eval_jaxpr/ppermute | solution.py:14
  219.6 6.1 %collective-permute-start = (f32[512]{0:T(512)S(1)}, f32[512]{0:T(512)S(1)}, u32[]{:S(2)}, u32[]{:S(2)}) collective-permute-start(f32[512]{0:T(512)S(1)} %add.85), channel_id=1, source_target_pairs={{0,2},{2,4},{4,6},{6,8},{8,10},{10,12},{12,14},{14,16},{16,18},{18... | collective-permute-start | bytes 6152 | tf_op jit(solution)/shard_map/while/body/eval_jaxpr/ppermute | solution.py:14
  232.4 6.1 %collective-permute-start = (f32[512]{0:T(512)S(1)}, f32[512]{0:T(512)S(1)}, u32[]{:S(2)}, u32[]{:S(2)}) collective-permute-start(f32[512]{0:T(512)S(1)} %add.85), channel_id=1, source_target_pairs={{0,2},{2,4},{4,6},{6,8},{8,10},{10,12},{12,14},{14,16},{16,18},{18... | collective-permute-start | bytes 6152 | tf_op jit(solution)/shard_map/while/body/eval_jaxpr/ppermute | solution.py:14
  245.3 6.1 %collective-permute-start = (f32[512]{0:T(512)S(1)}, f32[512]{0:T(512)S(1)}, u32[]{:S(2)}, u32[]{:S(2)}) collective-permute-start(f32[512]{0:T(512)S(1)} %add.85), channel_id=1, source_target_pairs={{0,2},{2,4},{4,6},{6,8},{8,10},{10,12},{12,14},{14,16},{16,18},{18... | collective-permute-start | bytes 6152 | tf_op jit(solution)/shard_map/while/body/eval_jaxpr/ppermute | solution.py:14
  258.1 6.1 %collective-permute-start = (f32[512]{0:T(512)S(1)}, f32[512]{0:T(512)S(1)}, u32[]{:S(2)}, u32[]{:S(2)}) collective-permute-start(f32[512]{0:T(512)S(1)} %add.85), channel_id=1, source_target_pairs={{0,2},{2,4},{4,6},{6,8},{8,10},{10,12},{12,14},{14,16},{16,18},{18... | collective-permute-start | bytes 6152 | tf_op jit(solution)/shard_map/while/body/eval_jaxpr/ppermute | solution.py:14
  270.9 6.1 %collective-permute-start = (f32[512]{0:T(512)S(1)}, f32[512]{0:T(512)S(1)}, u32[]{:S(2)}, u32[]{:S(2)}) collective-permute-start(f32[512]{0:T(512)S(1)} %add.85), channel_id=1, source_target_pairs={{0,2},{2,4},{4,6},{6,8},{8,10},{10,12},{12,14},{14,16},{16,18},{18... | collective-permute-start | bytes 6152 | tf_op jit(solution)/shard_map/while/body/eval_jaxpr/ppermute | solution.py:14
  283.8 6.1 %collective-permute-start = (f32[512]{0:T(512)S(1)}, f32[512]{0:T(512)S(1)}, u32[]{:S(2)}, u32[]{:S(2)}) collective-permute-start(f32[512]{0:T(512)S(1)} %add.85), channel_id=1, source_target_pairs={{0,2},{2,4},{4,6},{6,8},{8,10},{10,12},{12,14},{14,16},{16,18},{18... | collective-permute-start | bytes 6152 | tf_op jit(solution)/shard_map/while/body/eval_jaxpr/ppermute | solution.py:14
  296.6 6.1 %collective-permute-start = (f32[512]{0:T(512)S(1)}, f32[512]{0:T(512)S(1)}, u32[]{:S(2)}, u32[]{:S(2)}) collective-permute-start(f32[512]{0:T(512)S(1)} %add.85), channel_id=1, source_target_pairs={{0,2},{2,4},{4,6},{6,8},{8,10},{10,12},{12,14},{14,16},{16,18},{18... | collective-permute-start | bytes 6152 | tf_op jit(solution)/shard_map/while/body/eval_jaxpr/ppermute | solution.py:14
  309.4 6.1 %collective-permute-start = (f32[512]{0:T(512)S(1)}, f32[512]{0:T(512)S(1)}, u32[]{:S(2)}, u32[]{:S(2)}) collective-permute-start(f32[512]{0:T(512)S(1)} %add.85), channel_id=1, source_target_pairs={{0,2},{2,4},{4,6},{6,8},{8,10},{10,12},{12,14},{14,16},{16,18},{18... | collective-permute-start | bytes 6152 | tf_op jit(solution)/shard_map/while/body/eval_jaxpr/ppermute | solution.py:14
  322.3 6.1 %collective-permute-start = (f32[512]{0:T(512)S(1)}, f32[512]{0:T(512)S(1)}, u32[]{:S(2)}, u32[]{:S(2)}) collective-permute-start(f32[512]{0:T(512)S(1)} %add.85), channel_id=1, source_target_pairs={{0,2},{2,4},{4,6},{6,8},{8,10},{10,12},{12,14},{14,16},{16,18},{18... | collective-permute-start | bytes 6152 | tf_op jit(solution)/shard_map/while/body/eval_jaxpr/ppermute | solution.py:14
  335.1 6.1 %collective-permute-start = (f32[512]{0:T(512)S(1)}, f32[512]{0:T(512)S(1)}, u32[]{:S(2)}, u32[]{:S(2)}) collective-permute-start(f32[512]{0:T(512)S(1)} %add.85), channel_id=1, source_target_pairs={{0,2},{2,4},{4,6},{6,8},{8,10},{10,12},{12,14},{14,16},{16,18},{18... | collective-permute-start | bytes 6152 | tf_op jit(solution)/shard_map/while/body/eval_jaxpr/ppermute | solution.py:14
  347.9 6.1 %collective-permute-start = (f32[512]{0:T(512)S(1)}, f32[512]{0:T(512)S(1)}, u32[]{:S(2)}, u32[]{:S(2)}) collective-permute-start(f32[512]{0:T(512)S(1)} %add.85), channel_id=1, source_target_pairs={{0,2},{2,4},{4,6},{6,8},{8,10},{10,12},{12,14},{14,16},{16,18},{18... | collective-permute-start | bytes 6152 | tf_op jit(solution)/shard_map/while/body/eval_jaxpr/ppermute | solution.py:14
  360.7 6.1 %collective-permute-start = (f32[512]{0:T(512)S(1)}, f32[512]{0:T(512)S(1)}, u32[]{:S(2)}, u32[]{:S(2)}) collective-permute-start(f32[512]{0:T(512)S(1)} %add.85), channel_id=1, source_target_pairs={{0,2},{2,4},{4,6},{6,8},{8,10},{10,12},{12,14},{14,16},{16,18},{18... | collective-permute-start | bytes 6152 | tf_op jit(solution)/shard_map/while/body/eval_jaxpr/ppermute | solution.py:14
  366.9 8.4 %copy-start.2 = (f32[512,1024]{1,0:T(8,128)S(1)}, f32[512,1024]{1,0:T(8,128)}, u32[]{:S(2)}) copy-start(f32[512,1024]{1,0:T(8,128)} %copy-done.1) | copy-start | bytes 6291460
Sparse Core Ops, SparseCore 0:
  93.7 14.2 all-gather.5
  123.1 14.8 all-gather.7
